TPU v7x, 256 devices: a whole 4x4x8 slice. The times are simulated.
256 devices in a mesh: section: 4 (over y), dp: 32 (over x, z), tensor: 2 (over core).
Axes of the slice: x: 4, y: 4, z: 8, core: 2. Of those that a mesh axis runs over, the one named last changes fastest.
Arguments:
- activations: bfloat16 [4, 32768, 5120], P('section', 'dp'), may hold values from -6 to 6
- cotangents: bfloat16 [4, 32768, 1024], P('section', 'dp', 'tensor'), may hold values from -25 to 25
- doc_ids: int32 [32, 1024], P('dp'), may hold values from 0 to 15, never falling along the last dimension, each value on 1 to 128 neighbouring positions
Outputs:
- clipped_grad: float32 [4, 5120, 1024], P('section', 'dp', 'tensor')
- clip_factor: float32 [32, 16], P('dp')
Inputs may be any that keep to these rules, and one draw needn't show every extreme that they name: `doc_ids`: in each row the numbers never fall, every number 0 to 15 occurs, and each document has 1 to 128 tokens, one exactly 128.
All inputs are finite; a program needn't handle non-finite values.
Results may differ from a plain program's by a relative error of at most 0.0003.
Values may be sent and summed in bfloat16 or wider, within the bound.
A program may use at most 128 MiB of HBM per device.

v0:
```python
import math

import jax
import jax.numpy as jnp
from jax import lax
from jax.sharding import PartitionSpec as P

D = 5120
KV = 1024
DOCS = 16
CLIP_TOK = 192


def entering(value, axis, join, neutral):
    count, mine = (lax.axis_size(axis), lax.axis_index(axis))
    pieces = lax.all_gather(value, axis)
    so_far = jnp.full_like(value, 0) + jnp.asarray(neutral, value.dtype)

    def turn(position, so_far):
        longer = join(so_far, pieces[position])
        return jnp.where(position < mine, longer, so_far)

    return lax.fori_loop(0, count - 1, turn, so_far)


def broadcast(value, axis, source):
    kept = jnp.where(lax.axis_index(axis) == source, value, 0).astype(value.dtype)
    return lax.psum(kept, axis)


def tile_rows(activ, cotan, doc_tok):
    length = activ.shape[0]
    count = length // 128
    act_tiles = activ.reshape(count, 128, activ.shape[1])
    cot_tiles = cotan.reshape(count, 128, cotan.shape[1])
    id_tiles = doc_tok.reshape(count, 128)
    act_diag = jnp.einsum("ntd,nsd->nts", act_tiles, act_tiles, preferred_element_type=jnp.float32)
    cot_diag = jnp.einsum("ntd,nsd->nts", cot_tiles, cot_tiles, preferred_element_type=jnp.float32)
    same_diag = id_tiles[:, :, None] == id_tiles[:, None, :]
    row_sums = jnp.sum(jnp.where(same_diag, act_diag * cot_diag, jnp.float32(0.0)), axis=2)
    act_next = jnp.einsum(
        "ntd,nsd->nts", act_tiles[:-1], act_tiles[1:], preferred_element_type=jnp.float32
    )
    cot_next = jnp.einsum(
        "ntd,nsd->nts", cot_tiles[:-1], cot_tiles[1:], preferred_element_type=jnp.float32
    )
    same_next = id_tiles[:-1, :, None] == id_tiles[1:, None, :]
    product = jnp.where(same_next, act_next * cot_next, jnp.float32(0.0))
    zero_row = jnp.zeros((1, 128), jnp.float32)
    row_sums = row_sums + jnp.concatenate([jnp.sum(product, axis=2), zero_row], axis=0)
    row_sums = row_sums + jnp.concatenate([zero_row, jnp.sum(product, axis=1)], axis=0)
    return row_sums.reshape(length)


def add_terms(earlier, later):
    return earlier + later


def per_device(activations, cotangents, doc_ids):
    activ = activations[0]
    cotan = cotangents[0]
    doc_tok = doc_ids[0]
    length = activ.shape[0]
    sections = lax.axis_size("section")
    doc_range = jnp.arange(DOCS, dtype=jnp.int32)
    one_hot = (doc_tok[:, None] == doc_range[None, :]).astype(jnp.float32)
    row_sums = tile_rows(activ, cotan, doc_tok)
    partial_norms = jnp.sum(one_hot * row_sums[:, None], axis=0)
    bound = math.sqrt(4.0 * CLIP_TOK * sections * D * KV)
    tensor_total = lax.psum(partial_norms, "tensor")
    before = entering(tensor_total, "section", add_terms, jnp.zeros_like(tensor_total))
    norm_sq = before + tensor_total
    local_factor = jnp.minimum(jnp.float32(1.0), bound * lax.rsqrt(norm_sq + 1e-06))
    clip_factor = broadcast(local_factor, "section", sections - 1)
    scale = 1.0 / math.sqrt(lax.axis_size("dp") * length)
    token_factor = jnp.sum(one_hot * clip_factor[None, :], axis=1) * scale
    scaled = (cotan.astype(jnp.float32) * token_factor[:, None]).astype(jnp.bfloat16)
    grad_block = lax.psum_scatter(
        lax.dot_general(
            activ, scaled, (((0,), (0,)), ((), ())), preferred_element_type=jnp.float32
        ),
        "dp",
        scatter_dimension=0,
        tiled=True,
    )
    return (grad_block[None], clip_factor[None])


def solution(mesh):
    return jax.shard_map(
        per_device,
        mesh=mesh,
        in_specs=(P("section", "dp", None), P("section", "dp", "tensor"), P("dp", None)),
        out_specs=(P("section", "dp", "tensor"), P("dp", None)),
        check_vma=False,
    )
```

profile of v0, /device:TPU:2, one launch (start us, length us, event | category | flops | bytes accessed | tf_op | source)
XLA Modules:
  0.0 334.4 jit_solution(2021406511518860381)
XLA Ops:
  7.2 0.0 reduce-scatter.4.cloned.1.call-start
  7.2 0.8 slice_reduce_fusion.1
  8.0 14.8 %fusion.12 = (bf16[1,896,5120]{2,1,0:T(8,128)(2,1)}, bf16[1,896,5120]{2,1,0:T(8,128)(2,1)}) fusion(bf16[1,1024,5120]{2,1,0:T(8,128)(2,1)} %param.5), kind=kLoop, calls=%fused_computation.22 | loop fusion | bytes 36700160 | tf_op jit(solution)/shard_map/slice | solution.py:42
  22.8 9.9 %fusion.14 = f32[8,128,128]{1,2,0:T(8,128)S(1)} fusion(bf16[8,128,5120]{2,1,0:T(8,128)(2,1)} %bitcast.38), kind=kOutput, calls=%fused_computation.24 | convolution fusion | flops 1342177280 | bytes 11010048 | tf_op jit(solution)/shard_map/ntd,nsd->nts/dot_general | solution.py:37
  32.7 0.1 fusion.13
  32.9 0.4 fusion.15
  33.3 0.0 copy-start.3
  33.3 0.4 fusion.7
  33.8 8.8 %fusion.11 = (f32[7,128]{1,0:T(8,128)S(1)}, f32[7,128]{1,0:T(8,128)S(1)}) fusion(f32[7,128,128]{2,1,0:T(8,128)S(1)} %fusion.15, bf16[7,128,5120]{2,1,0:T(8,128)(2,1)} %bitcast.40, bf16[7,128,5120]{2,1,0:T(8,128)(2,1)} %bitcast.39, s32[7,128]{1,0:T(8,128)S(1)} %bitcast.49, s32[7,128]{1,0:T(8,128)S(1)} %bitcast.48), kind=kOutput, calls=%fused_computation.21 | convolution fusion | flops 1174976768 | bytes 18823168 | tf_op jit(solution)/shard_map/ntd,nsd->nts/dot_general | solution.py:41
  42.6 0.1 select_reduce_fusion.1
  42.8 2.5 psum.14
  45.2 0.7 dynamic-slice
  46.6 0.2 dynamic-update-slice
  46.8 10.7 %all-reduce.2 = f32[64]{0:T(128)S(1)} all-reduce(f32[64]{0:T(128)S(1)} %dynamic-update-slice), channel_id=2, replica_groups=mesh['section'=4,'dp'=32,'tensor'=2] {'section'}, use_global_device_ids=true, to_apply=%add.2 | all-reduce | flops 64 | bytes 512
  57.6 0.1 reshape.30
  57.6 0.1 while.14
  57.8 7.7 %psum.15 = f32[16]{0:T(128)S(1)} all-reduce(f32[16]{0:T(128)S(1)} %broadcast_select_fusion.2), channel_id=1, replica_groups=mesh['section'=4,'dp'=32,'tensor'=2] {'section'}, use_global_device_ids=true, to_apply=%region_7.8 | all-reduce | flops 16 | bytes 128 | tf_op jit(solution)/shard_map/psum | solution.py:28
  65.5 0.1 select_reduce_fusion
  65.6 12.3 %fusion.2 = f32[5120,512]{0,1:T(8,128)} fusion(bf16[1,1024,5120]{2,1,0:T(8,128)(2,1)} %param.5, bf16[1,1024,512]{2,1,0:T(8,128)(2,1)S(1)} %copy-done, f32[1024]{0:T(1024)S(1)} %broadcast_multiply_fusion), kind=kOutput, calls=%fused_computation.4 | convolution fusion | flops 5370281984 | bytes 22024192 | tf_op jit(solution)/shard_map/dot_general | solution.py:79
  77.9 11.4 %copy.8 = f32[5120,512]{1,0:T(8,128)} copy(f32[5120,512]{0,1:T(8,128)} %fusion.2) | data formatting | bytes 20971520
  89.3 0.0 reduce-scatter.4.cloned.1.call-update
  89.3 236.2 %reduce-scatter.4.cloned.1.call-done = f32[160,512]{1,0:T(8,128)} async-done(((f32[5120,512]{1,0:T(8,128)}), f32[160,512]{1,0:T(8,128)}) %reduce-scatter.4.cloned.1.call-update) | async-done | bytes 327696
  325.5 1.2 copy.9
  326.7 0.9 copy.7
  (15 shorter events, 0.1 us)
Async XLA Ops:
  7.2 318.3 %reduce-scatter.4.cloned.1.call-start = ((), (), s32[]{:S(2)}) async-start(), calls=%async_computation.1 | async-start | bytes 10813440
  22.8 9.9 %copy-start = (bf16[1,1024,512]{2,1,0:T(8,128)(2,1)S(1)}, bf16[1,1024,512]{2,1,0:T(8,128)(2,1)}, u32[]{:S(2)}) copy-start(bf16[1,1024,512]{2,1,0:T(8,128)(2,1)} %param.6) | copy-start | bytes 3145732
  22.8 10.5 %copy-start.1 = (s32[1,1024]{1,0:T(1,128)S(1)}, s32[1,1024]{1,0:T(1,128)}, u32[]{:S(2)}) copy-start(s32[1,1024]{1,0:T(1,128)} %param.7) | copy-start | bytes 12292
  33.3 11.9 %copy-start.3 = (u32[256]{0:T(256)S(1)}, u32[256]{0:T(256)}, u32[]{:S(2)}) copy-start(u32[256]{0:T(256)} %constant.56) | copy-start | bytes 3076
  65.5 12.4 %copy-start.2 = (f32[16]{0:T(128)}, f32[16]{0:T(128)S(1)}, u32[]{:S(2)}) copy-start(f32[16]{0:T(128)S(1)} %psum.15) | copy-start | bytes 196
Sparse Core Ops, SparseCore 0:
  89.4 236.0 reduce-scatter.3
where the time goes:
time: 335 us; the launch traced here: 334 us
  waiting for transfers between devices  236 us (70%)
  matrix products  31.9 us (10%)
  local copies, waits for them, and re-layouts  30.2 us (9%)
  blocking collectives  20.9 us (6%)
  between operations  14.9 us (4%)
    unnamed x2, waiting for transfers between devices  236 us
    slice x1, local copies, waits for them, and re-layouts, tile_rows(): act_tiles[1:]  14.8 us
    unnamed x14, local copies, waits for them, and re-layouts  14.4 us
    dot_general x1, matrix products, per_device(): lax.dot_general(activ, scaled, (((0,), (0,)), ((), ())), preferred_elemen...  12.3 us
    unnamed x1, blocking collectives  10.7 us
    dot_general x1, matrix products, tile_rows(): jnp.einsum('ntd,nsd->nts', act_tiles, act_tiles, preferred_element_type=j...  9.91 us
    dot_general x1, matrix products, tile_rows(): jnp.einsum('ntd,nsd->nts', act_tiles[:-1], act_tiles[1:], preferred_eleme...  8.85 us
    psum x1, blocking collectives, broadcast(): return lax.psum(kept, axis)  7.75 us
  transfers between devices with their start and end apart: 1, of which 1 were waited for; matrix products, arithmetic and copies ran while one was open for 0% of the time, Pallas kernels for 0%

commit v1 on v0

v1 whole, which is shorter than its diff:
```python
import functools
import math

import jax
import jax.numpy as jnp
from jax import lax
from jax.experimental import pallas as pl
from jax.experimental.pallas import tpu as pltpu
from jax.sharding import PartitionSpec as P

D = 5120
KV = 1024
DOCS = 16
CLIP_TOK = 192

F32 = jnp.float32
BF16 = jnp.bfloat16
I16 = jnp.int16
MESH = pl.DeviceIdType.MESH
TOP = 32767.0
TINY = 1e-30

NX, NZ = 4, 8
BLOCK = D // (NX * NZ)
ROWS1, ROWS2 = 96, 64
H1, H2 = ROWS1 // 2, ROWS2 // 2
STEPS = NZ
LAG_B, LAG_C = 2, 4


def nt(a, b):
    return lax.dot_general(a, b, (((1,), (1,)), ((), ())), preferred_element_type=F32)


def tn(a, b, precision=None):
    return lax.dot_general(a, b, (((0,), (0,)), ((), ())), preferred_element_type=F32, precision=precision)


def zeta(z, p):
    odd = p % 2
    return (z + 4 + (1 - odd) * (p // 2) - odd * ((p + 1) // 2)) % NZ


def kernel(
    a_hbm, g_hbm, ids_ref, out_ref, clip_ref,
    a, at, g, gp, part, scaled, norms,
    xs1, xr1, xss1, xrs1, zs1, zr1, zss1, zrs1,
    xs2, xr2, xss2, xrs2, zs2, zr2, zss2, zrs2,
    a_sem, g_sem, gp_send, gp_recv, n_send, n_recv,
    x1_send, x1_recv, z1_send, z1_recv, x2_send, x2_recv, z2_send, z2_recv,
):
    length = a.shape[0]
    sections = lax.axis_size("section")
    y, dp, core = lax.axis_index("section"), lax.axis_index("dp"), lax.axis_index("tensor")
    x, z = dp // NZ, dp % NZ

    def at_x(step):
        return (y, ((x + step) % NX) * NZ + z, core)

    def at_z(step):
        return (y, x * NZ + (z + step) % NZ, core)

    group = [((y + i) % sections, dp, (core + j) % 2) for i in range(4) for j in range(2) if i or j]
    barrier = pltpu.get_barrier_semaphore()
    for peer in group + [at_x(1), at_x(NX - 1), at_z(1), at_z(NZ - 1)]:
        pl.semaphore_signal(barrier, inc=1, device_id=peer, device_id_type=MESH)

    chunks = length // 128

    def a_copy(i):
        row = pl.multiple_of(((i + 3 * core) % chunks) * 128, 128)
        return pltpu.make_async_copy(a_hbm.at[pl.ds(row, 128)], a.at[pl.ds(row, 128)], a_sem.at[i])

    g_copy = pltpu.make_async_copy(g_hbm, g, g_sem)
    g_copy.start()
    for i in range(chunks):
        a_copy(i).start()
    pl.semaphore_wait(barrier, len(group) + 4)

    other_row = pl.multiple_of(384 * (1 - core), 128)
    gp_copy = pltpu.make_async_remote_copy(
        g_hbm.at[pl.ds(other_row, 640)], gp.at[pl.ds(other_row, 640)], gp_send, gp_recv,
        device_id=(y, dp, 1 - core), device_id_type=MESH,
    )
    gp_copy.start()

    one_hot = (lax.broadcasted_iota(jnp.int32, (DOCS, length), 0) == ids_ref[...]).astype(F32)

    hot_ref = norms.at[2 * sections]
    for k in range(length // 128):
        norms[2 * sections + k] = one_hot[:, k * 128 : (k + 1) * 128]
    del hot_ref

    def hot(first, count):
        return jnp.concatenate([norms[2 * sections + first + k] for k in range(count)], axis=1)

    g_copy.wait()
    for i in range(3):
        a_copy(i).wait()
    total = jnp.zeros((DOCS, 256), F32)
    for j in range(2):
        if j == 1:
            for i in range(3, 5):
                a_copy(i).wait()
        u0 = pl.multiple_of(512 * core + 256 * j, 128)
        t0 = pl.multiple_of(jnp.maximum(u0 - 128, 0), 128)
        act = nt(a[pl.ds(t0, 384), :], a[pl.ds(u0, 256), :])
        if j == 0:
            gp_copy.wait_recv()
        cot = nt(g[pl.ds(t0, 384), :], g[pl.ds(u0, 256), :]) + nt(gp[pl.ds(t0, 384), :], gp[pl.ds(u0, 256), :])
        hot_u = hot(u0 // 128, 2)
        same = tn(hot(t0 // 128, 3), hot_u)
        t = lax.broadcasted_iota(jnp.int32, (384, 256), 0) + t0
        weight = jnp.where(t < u0, 2.0, jnp.where(t < u0 + 256, 1.0, 0.0))
        product = jnp.where(same > 0.5, act * cot * weight, 0.0)
        total = total + hot_u * jnp.sum(product, axis=0, keepdims=True)
    mine = y * 2 + core
    norms[mine] = total[:, :128] + total[:, 128:]
    n_copies = [
        pltpu.make_async_remote_copy(
            norms.at[mine], norms.at[mine], n_send.at[i], n_recv.at[i], device_id=peer, device_id_type=MESH
        )
        for i, peer in enumerate(group)
    ]
    for copy in n_copies:
        copy.start()

    for i in range(5, chunks):
        a_copy(i).wait()

    def transpose(i, _):
        lane = pl.multiple_of(i * 128, 128)
        at[pl.ds(lane, 128), :] = a[:, pl.ds(lane, 128)].T
        return 0

    lax.fori_loop(0, D // 128, transpose, 0)

    for copy in n_copies:
        copy.wait_recv()
    norm_sq = norms[0]
    for i in range(1, 2 * sections):
        norm_sq = norm_sq + norms[i]
    norm_sq = jnp.broadcast_to(jnp.sum(norm_sq, axis=1, keepdims=True), (DOCS, 128))
    bound = math.sqrt(4.0 * CLIP_TOK * sections * D * KV)
    clip = jnp.minimum(1.0, bound * lax.rsqrt(norm_sq + 1e-06))
    clip_ref[...] = clip.T[:1, :]
    factor = clip * (1.0 / math.sqrt(NX * NZ * length))
    for k in range(length // 128):
        fac = tn(norms[2 * sections + k], factor, lax.Precision.HIGHEST)
        for lane in range(0, KV // 2, 128):
            own = g[k * 128 : (k + 1) * 128, lane : lane + 128].astype(F32)
            scaled[k * 128 : (k + 1) * 128, lane : lane + 128] = (own * fac).astype(BF16)

    def base(x_of, z_of):
        return (x_of * NZ + z_of) * BLOCK

    def multiply(p):
        def one(i, _):
            row = pl.multiple_of(base(i, zeta(z, p)), 32)
            part[pl.ds(row, BLOCK), :] = jnp.dot(at[pl.ds(row, BLOCK), :], scaled[...], preferred_element_type=F32)
            return 0

        lax.fori_loop(0, NX, one, 0)

    def pieces(rows):
        return range(0, rows, 16)

    def decode(code, scale):
        return code.astype(jnp.int32).astype(F32) * scale

    def fold(m, value):
        value = jnp.abs(value)
        for r in range(0, value.shape[0], 8):
            for c in range(0, value.shape[1], 128):
                m = jnp.maximum(m, value[r : r + 8, c : c + 128])
        return m

    def spread(scale, like):
        return jnp.concatenate([scale] * (like // 128), axis=1)

    def encode(rows, count, code, scale_ref, add=None):
        m = jnp.zeros((8, 128), F32)
        for b, row in enumerate(rows):
            for r in pieces(count):
                value = part[pl.ds(pl.multiple_of(row + r, 16), 16), :]
                if add is not None:
                    value = value + add(b, r)
                    part[pl.ds(pl.multiple_of(row + r, 16), 16), :] = value
                m = fold(m, value)
        m = jnp.maximum(jnp.max(m, axis=0, keepdims=True), TINY)
        scale_ref[...] = jnp.broadcast_to(m * (1.0 / TOP), (8, 128))
        inverse = spread(TOP / m, KV // 2)
        for b, row in enumerate(rows):
            for r in pieces(count):
                value = part[pl.ds(pl.multiple_of(row + r, 16), 16), :]
                code[b * count + r : b * count + r + 16, :] = jnp.round(value * inverse).astype(jnp.int32).astype(I16)

    def adder(count, code, scale_ref):
        scale = spread(scale_ref[0:1, :], KV // 2)
        return lambda b, r: decode(code[b * count + r : b * count + r + 16, :], scale)

    def send(code, scale, to_code, to_scale, send_sem, recv_sem, peer):
        return (
            pltpu.make_async_remote_copy(code, to_code, send_sem.at[0], recv_sem.at[0], device_id=peer, device_id_type=MESH),
            pltpu.make_async_remote_copy(
                scale, to_scale, send_sem.at[1], recv_sem.at[1], device_id=peer, device_id_type=MESH
            ),
        )

    def start(copies):
        for copy in copies:
            copy.start()

    def landed(copies):
        for copy in copies:
            copy.wait_recv()

    class Ring:
        def __init__(self, half, first, bufs, sems):
            self.half, self.first = half, first
            self.code, self.got, self.scale, self.got_scale = bufs
            self.send_sem, self.recv_sem = sems

        def copies(self, p, way, unit):
            return send(
                self.code.at[p, way, unit], self.scale.at[p, way, unit, 0:1],
                self.got.at[p, way, unit], self.got_scale.at[p, way, unit, 0:1],
                self.send_sem.at[p, way, unit], self.recv_sem.at[p, way, unit], at_x(1 if way == 0 else NX - 1),
            )

        def row(self, step, z_of, half):
            return base((x + step) % NX, z_of) + self.first + half * self.half

        def own(self, p, z_of):
            for unit in range(2):
                for way in range(2):
                    step = 2 if unit == 0 else (1 if way == 0 else NX - 1)
                    half = way if unit == 0 else 1 - way
                    encode(
                        [self.row(step, z_of, half)], self.half, self.code.at[p, way, unit], self.scale.at[p, way, unit]
                    )
                    start(self.copies(p, way, unit))

        def pass_on(self, p, z_of):
            for way in range(2):
                landed(self.copies(p, way, 0))
                encode(
                    [self.row(1 if way == 0 else NX - 1, z_of, way)], self.half,
                    self.code.at[p, way, 2], self.scale.at[p, way, 2],
                    adder(self.half, self.got.at[p, way, 0], self.got_scale.at[p, way, 0]),
                )
                start(self.copies(p, way, 2))

        def finish(self, p, z_of, put):
            for unit in (1, 2):
                for way in range(2):
                    landed(self.copies(p, way, unit))
            for half in range(2):
                one = adder(self.half, self.got.at[p, half, 2], self.got_scale.at[p, half, 2])
                two = adder(self.half, self.got.at[p, 1 - half, 1], self.got_scale.at[p, 1 - half, 1])
                row = self.row(0, z_of, half)
                for r in pieces(self.half):
                    value = part[pl.ds(pl.multiple_of(row + r, 16), 16), :] + one(0, r) + two(0, r)
                    put(row, half, r, value)

        def drain(self, steps):
            def one(p, _):
                for way in range(2):
                    for unit in range(3):
                        for copy in self.copies(p, way, unit):
                            copy.wait_send()
                return 0

            lax.fori_loop(0, steps, one, 0)

    class Chain:
        def __init__(self, half, first, blocks, bufs, sems):
            self.half, self.first, self.blocks = half, first, blocks
            self.code, self.got, self.scale, self.got_scale = bufs
            self.send_sem, self.recv_sem = sems

        def rows(self, z_of, half):
            return [base(b, z_of) + self.first + half * self.half for b in self.blocks]

        def copies(self, p, half, slot, step):
            return send(
                self.code.at[p, half], self.scale.at[p, half, 0:1], self.got.at[slot, half], self.got_scale.at[slot, half, 0:1],
                self.send_sem.at[p, half], self.recv_sem.at[slot, half], at_z(step),
            )

        def clear(self):
            for slot, half in ((0, 1), (1, 0)):
                self.got_scale[slot, half] = jnp.zeros((8, 128), F32)

        def begin(self):
            for half in range(2):
                encode(self.rows(zeta(z, 0), half), self.half, self.code.at[0, half], self.scale.at[0, half])
                start(self.copies(0, half, half, 1 if half == 0 else NZ - 1))

        def step(self, p):
            odd = p % 2
            for half in (odd, 1 - odd):

                def arrived(half=half):
                    landed(self.copies(p, half, p - 1, 1))

                if half is odd:
                    pl.when(p >= 3)(arrived)
                else:
                    arrived()
                encode(
                    self.rows(zeta(z, p), half), self.half, self.code.at[p, half], self.scale.at[p, half],
                    adder(self.half, self.got.at[p - 1, half], self.got_scale.at[p - 1, half]),
                )
                start(self.copies(p, half, p + 1, 1 + (1 - odd) * (NZ - 2)))

        def finish(self, put):
            for slot in (NZ - 2, NZ - 1):
                for half in range(2):
                    landed(self.copies(0, half, slot, 1))
            for half in range(2):
                one = adder(self.half, self.got.at[NZ - 2, half], self.got_scale.at[NZ - 2, half])
                two = adder(self.half, self.got.at[NZ - 1, half], self.got_scale.at[NZ - 1, half])
                for b, row in enumerate(self.rows(z, half)):
                    for r in pieces(self.half):
                        value = part[pl.ds(pl.multiple_of(row + r, 16), 16), :] + one(b, r) + two(b, r)
                        put(row, half, r, value)

        def drain(self):
            def one(p, _):
                for half in range(2):
                    for copy in self.copies(p, half, 0, 1):
                        copy.wait_send()
                return 0

            lax.fori_loop(0, NZ - 1, one, 0)

    ring1 = Ring(H1, 0, (xs1, xr1, xss1, xrs1), (x1_send, x1_recv))
    chain1 = Chain(H1, 0, [x], (zs1, zr1, zss1, zrs1), (z1_send, z1_recv))
    ring2 = Ring(H2, ROWS1, (xs2, xr2, xss2, xrs2), (x2_send, x2_recv))
    chain2 = Chain(H2, ROWS1, list(range(NX)), (zs2, zr2, zss2, zrs2), (z2_send, z2_recv))

    def keep(row, half, r, value):
        part[pl.ds(pl.multiple_of(row + r, 16), 16), :] = value

    def put1(row, half, r, value):
        out_ref[half * H1 + r : half * H1 + r + 16, :] = value

    def put2(row, half, r, value):
        out_ref[ROWS1 + half * H2 + r : ROWS1 + half * H2 + r + 16, :] = value

    chain1.clear()
    chain2.clear()

    def turn(s, _):
        @pl.when(s < STEPS)
        def _():
            multiply(s)
            ring1.own(s, zeta(z, s))

        pl.when(s == 0)(chain2.begin)

        @pl.when((s >= 1) & (s <= STEPS - 2))
        def _():
            chain2.step(s)

        @pl.when(s == STEPS - 1)
        def _():
            chain2.finish(keep)
            ring2.own(0, z)

        @pl.when((s >= LAG_B) & (s < STEPS + LAG_B))
        def _():
            ring1.pass_on(s - LAG_B, zeta(z, s - LAG_B))

        pl.when(s == STEPS)(lambda: ring2.pass_on(0, z))
        pl.when(s == STEPS + 1)(lambda: ring2.finish(0, z, put2))

        @pl.when(s >= LAG_C)
        def _():
            ring1.finish(s - LAG_C, zeta(z, s - LAG_C), keep)

        pl.when(s == LAG_C)(chain1.begin)

        @pl.when((s > LAG_C) & (s < STEPS + LAG_C - 1))
        def _():
            chain1.step(s - LAG_C)

        return 0

    lax.fori_loop(0, STEPS + LAG_C, turn, 0)
    chain1.finish(put1)

    gp_copy.wait_send()
    for copy in n_copies:
        copy.wait_send()
    ring1.drain(STEPS)
    chain1.drain()
    ring2.drain(1)
    chain2.drain()


def per_device(activations, cotangents, doc_ids):
    length, half_kv = activations.shape[1], cotangents.shape[2]
    sections = lax.axis_size("section")
    dma = pltpu.SemaphoreType.DMA
    units1, units2 = (STEPS, 2, 3), (1, 2, 3)
    hops = (STEPS, 2)

    def buffers(shape, rows):
        return [pltpu.VMEM(shape + (rows, half_kv), I16)] * 2 + [pltpu.VMEM(shape + (8, 128), F32)] * 2

    grad, clip = pl.pallas_call(
        kernel,
        out_shape=(
            jax.ShapeDtypeStruct((BLOCK, half_kv), F32),
            jax.ShapeDtypeStruct((1, DOCS), F32),
        ),
        in_specs=[
            pl.BlockSpec(memory_space=pl.ANY),
            pl.BlockSpec(memory_space=pl.ANY),
            pl.BlockSpec(memory_space=pltpu.VMEM),
        ],
        out_specs=[pl.BlockSpec(memory_space=pltpu.VMEM)] * 2,
        scratch_shapes=[
            pltpu.VMEM((length, D), BF16),
            pltpu.VMEM((D, length), BF16),
            pltpu.VMEM((length, half_kv), BF16),
            pltpu.VMEM((length, half_kv), BF16),
            pltpu.VMEM((D, half_kv), F32),
            pltpu.VMEM((length, half_kv), BF16),
            pltpu.VMEM((2 * sections + length // 128, DOCS, 128), F32),
            *buffers(units1, H1),
            *buffers(hops, H1),
            *buffers(units2, H2),
            *buffers(hops, NX * H2),
            dma((length // 128,)),
            dma(()),
            dma(()),
            dma(()),
            dma((7,)),
            dma((7,)),
            dma(units1 + (2,)),
            dma(units1 + (2,)),
            dma(hops + (2,)),
            dma(hops + (2,)),
            dma(units2 + (2,)),
            dma(units2 + (2,)),
            dma(hops + (2,)),
            dma(hops + (2,)),
        ],
        compiler_params=pltpu.CompilerParams(
            collective_id=0, has_side_effects=True, vmem_limit_bytes=63 << 20
        ),
        name="clip_and_reduce",
    )(activations[0], cotangents[0], doc_ids)
    return grad[None], clip


def solution(mesh):
    return jax.shard_map(
        per_device,
        mesh=mesh,
        in_specs=(P("section", "dp", None), P("section", "dp", "tensor"), P("dp", None)),
        out_specs=(P("section", "dp", "tensor"), P("dp", None)),
        check_vma=False,
    )
```

time: 335 us -> 69.9 us (0.21)
  waiting for transfers between devices: 236 us -> 0 us
  Pallas kernels: 0 us -> 66.3 us
  matrix products: 31.9 us -> 0 us
  local copies, waits for them, and re-layouts: 30.2 us -> 2.83 us
  blocking collectives: 20.9 us -> 0 us
  between operations: 14.9 us -> 0.64 us
    unnamed x2 -> x0, waiting for transfers between devices: 236 us -> none
    pallas_call x0 -> x1, Pallas kernels: none -> 66.3 us  [per_device(): pl.pallas_call(kernel, out_shape=(jax.ShapeDtypeStruct((BLOCK, half_kv),...]
    dot_general x5 -> x0, matrix products: 31.9 us -> none  [the longest x1 12.3 us: per_device(): lax.dot_general(activ, scaled, (((0,), (0,)), ((), ())), preferred_elemen...]
    slice x3 -> x0, local copies, waits for them, and re-layouts: 15.7 us -> none  [the longest x1 14.8 us: tile_rows(): act_tiles[1:]]
    unnamed x14 -> x2, local copies, waits for them, and re-layouts: 14.4 us -> 2.83 us
    unnamed x1 -> x0, blocking collectives: 10.7 us -> none
    psum x2 -> x0, blocking collectives: 10.2 us -> none  [the longest x1 7.75 us: broadcast(): return lax.psum(kept, axis)]
  transfers between devices with their start and end apart: 1 -> 0, of which waited for: 1 -> 0; matrix products, arithmetic and copies ran while one was open for 0% -> 0% of each run, Pallas kernels for 0% -> 0%
where the time goes in v1:
time: 69.9 us; the launch traced here: 69.7 us
  Pallas kernels  66.3 us (95%)
  local copies, waits for them, and re-layouts  2.83 us (4%)
    pallas_call x1, Pallas kernels, per_device(): pl.pallas_call(kernel, out_shape=(jax.ShapeDtypeStruct((BLOCK, half_kv),...  66.3 us
    unnamed x2, local copies, waits for them, and re-layouts  2.83 us

profile of v1, /device:TPU:2, one launch (start us, length us, event | category | flops | bytes accessed | tf_op | source)
XLA Modules:
  0.0 69.7 jit_solution(7384321777005323204)
XLA Ops:
  0.6 66.3 %clip_and_reduce.1 = (f32[160,512]{1,0:T(8,128)}, f32[1,16]{1,0:T(1,128)}) custom-call(bf16[1024,5120]{1,0:T(8,128)(2,1)} %bitcast.3, bf16[1024,512]{1,0:T(8,128)(2,1)} %bitcast.4, s32[1,1024]{1,0:T(1,128)} %ids_ref.1), custom_call_target="tpu_custom_call" | custom-call | tf_op jit(solution)/shard_map/clip_and_reduce/pallas_call | solution.py:413
  66.9 1.7 %copy.7 = f32[1,160,512]{2,1,0:T(8,128)} copy(f32[1,160,512]{2,1,0:T(8,128)} %bitcast.5) | data formatting | bytes 655360
  68.6 1.1 %copy.8 = f32[1,16]{1,0:T(1,128)} copy(f32[1,16]{1,0:T(1,128)} %get-tuple-element.9) | data formatting | bytes 128

commit v2 on v1

v2 whole, which is shorter than its diff:
```python
import functools
import math

import jax
import jax.numpy as jnp
from jax import lax
from jax.experimental import pallas as pl
from jax.experimental.pallas import tpu as pltpu
from jax.sharding import PartitionSpec as P

D = 5120
KV = 1024
DOCS = 16
CLIP_TOK = 192

F32 = jnp.float32
BF16 = jnp.bfloat16
I16 = jnp.int16
MESH = pl.DeviceIdType.MESH
TOP = 32767.0
TINY = 1e-30

NX, NZ = 4, 8
BLOCK = D // (NX * NZ)
ROWS1, ROWS2 = 96, 64
H1, H2 = ROWS1 // 2, ROWS2 // 2
STEPS = NZ
K_CHUNK = 1280
TRANSPOSE_EARLY = True
ORDER = (
    "M0", "A0", "H00", "M1", "H10", "A1", "M2", "H20", "A2", "M3", "B0", "A3", "M4", "H11", "H21", "A4", "M5", "B1", "M6",
    "H30", "B2", "A5", "H40", "M7", "C0", "Z0", "A7", "A6", "H31", "H41", "B3", "H50", "H60", "B4", "C1", "Z1", "C2", "Z2",
    "H51", "H61", "B5", "B7", "B6", "C3", "Z3", "C4", "Z4", "E", "F", "C5", "C7", "Z5", "C6", "Z6", "G", "I",
)


def nt(a, b):
    return lax.dot_general(a, b, (((1,), (1,)), ((), ())), preferred_element_type=F32)


def tn(a, b, precision=None):
    return lax.dot_general(a, b, (((0,), (0,)), ((), ())), preferred_element_type=F32, precision=precision)


def zeta(z, p):
    odd = p % 2
    return (z + 4 + (1 - odd) * (p // 2) - odd * ((p + 1) // 2)) % NZ


def kernel(
    a_hbm, g_hbm, ids_ref, out_ref, clip_ref,
    a, at, g, gp, part, scaled, norms, acts, cots,
    xs1, xr1, xss1, xrs1, zs1, zr1, zss1, zrs1,
    xs2, xr2, xss2, xrs2, zs2, zr2, zss2, zrs2,
    a_sem, g_sem, gp_sem, n_send, n_recv, sent, x1_recv, z1_recv, x2_recv, z2_recv,
):
    length = a.shape[0]
    sections = lax.axis_size("section")
    y, dp, core = lax.axis_index("section"), lax.axis_index("dp"), lax.axis_index("tensor")
    x, z = dp // NZ, dp % NZ

    def at_x(step):
        return (y, ((x + step) % NX) * NZ + z, core)

    def at_z(step):
        return (y, x * NZ + (z + step) % NZ, core)

    group = [((y + i) % sections, dp, (core + j) % 2) for i in range(4) for j in range(2) if i or j]
    barrier = pltpu.get_barrier_semaphore()
    for peer in group + [at_x(1), at_x(NX - 1), at_z(1), at_z(NZ - 1)]:
        pl.semaphore_signal(barrier, inc=1, device_id=peer, device_id_type=MESH)

    chunks = D // K_CHUNK
    first = pl.multiple_of(384 * core, 128)
    rest = pl.multiple_of(640 * (1 - core), 128)

    def a_copy(k):
        if k < chunks:
            where = (pl.ds(first, 640), pl.ds(k * K_CHUNK, K_CHUNK))
        else:
            where = (pl.ds(pl.multiple_of(rest + 128 * (k - chunks), 128), 128), pl.ds(0, D))
        return pltpu.make_async_copy(a_hbm.at[where], a.at[where], a_sem.at[k])

    g_copy = pltpu.make_async_copy(g_hbm, g, g_sem)
    g_copy.start()
    for k in range(2):
        a_copy(k).start()
    pl.semaphore_wait(barrier, len(group) + 4)

    other_row = pl.multiple_of(384 * (1 - core), 128)
    gp_copy = pltpu.make_async_remote_copy(
        g_hbm.at[pl.ds(other_row, 640)], gp.at[pl.ds(other_row, 640)], gp_sem.at[0], gp_sem.at[1],
        device_id=(y, dp, 1 - core), device_id_type=MESH,
    )
    gp_copy.start()

    one_hot = (lax.broadcasted_iota(jnp.int32, (DOCS, length), 0) == ids_ref[...]).astype(F32)
    for k in range(length // 128):
        norms[2 * sections + k] = one_hot[:, k * 128 : (k + 1) * 128]

    def hot(start, count):
        return jnp.concatenate([norms[2 * sections + start + k] for k in range(count)], axis=1)

    def tokens(j):
        u0 = pl.multiple_of(512 * core + 256 * j, 128)
        return pl.multiple_of(jnp.maximum(u0 - 128, 0), 128), u0

    g_copy.wait()
    for j in range(2):
        t0, u0 = tokens(j)
        cots[j] = nt(g[pl.ds(t0, 384), :], g[pl.ds(u0, 256), :])

    for k in range(chunks):
        a_copy(k).wait()
        if k + 2 < chunks:
            a_copy(k + 2).start()
        elif k + 2 == chunks:
            for i in range(3):
                a_copy(chunks + i).start()
        column = k * K_CHUNK
        for j in range(2):
            t0, u0 = tokens(j)
            product = nt(a[pl.ds(t0, 384), pl.ds(column, K_CHUNK)], a[pl.ds(u0, 256), pl.ds(column, K_CHUNK)])
            acts[j] = product if k == 0 else acts[j] + product
        for lane in range(column, column + K_CHUNK, 128) if TRANSPOSE_EARLY else ():
            at[lane : lane + 128, pl.ds(first, 640)] = a[pl.ds(first, 640), lane : lane + 128].T

    gp_copy.wait_recv()
    total = jnp.zeros((DOCS, 256), F32)
    for j in range(2):
        t0, u0 = tokens(j)
        cot = cots[j] + nt(gp[pl.ds(t0, 384), :], gp[pl.ds(u0, 256), :])
        hot_u = hot(u0 // 128, 2)
        same = tn(hot(t0 // 128, 3), hot_u)
        t = lax.broadcasted_iota(jnp.int32, (384, 256), 0) + t0
        weight = jnp.where(t < u0, 2.0, jnp.where(t < u0 + 256, 1.0, 0.0))
        product = jnp.where(same > 0.5, acts[j] * cot * weight, 0.0)
        total = total + hot_u * jnp.sum(product, axis=0, keepdims=True)
    mine = y * 2 + core
    norms[mine] = total[:, :128] + total[:, 128:]
    n_copies = [
        pltpu.make_async_remote_copy(
            norms.at[mine], norms.at[mine], n_send, n_recv.at[i], device_id=peer, device_id_type=MESH
        )
        for i, peer in enumerate(group)
    ]
    for copy in n_copies:
        copy.start()

    for i in range(3):
        a_copy(chunks + i).wait()

    def transpose(i, _):
        lane = pl.multiple_of(i * 128, 128)
        if not TRANSPOSE_EARLY:
            at[pl.ds(lane, 128), pl.ds(first, 640)] = a[pl.ds(first, 640), pl.ds(lane, 128)].T
        at[pl.ds(lane, 128), pl.ds(rest, 384)] = a[pl.ds(rest, 384), pl.ds(lane, 128)].T
        return 0

    lax.fori_loop(0, D // 128, transpose, 0)

    for copy in n_copies:
        copy.wait_recv()
    norm_sq = norms[0]
    for i in range(1, 2 * sections):
        norm_sq = norm_sq + norms[i]
    norm_sq = jnp.broadcast_to(jnp.sum(norm_sq, axis=1, keepdims=True), (DOCS, 128))
    bound = math.sqrt(4.0 * CLIP_TOK * sections * D * KV)
    clip = jnp.minimum(1.0, bound * lax.rsqrt(norm_sq + 1e-06))
    clip_ref[...] = clip.T[:1, :]
    factor = clip * (1.0 / math.sqrt(NX * NZ * length))
    for k in range(length // 128):
        fac = tn(norms[2 * sections + k], factor, lax.Precision.HIGHEST)
        for lane in range(0, KV // 2, 128):
            own = g[k * 128 : (k + 1) * 128, lane : lane + 128].astype(F32)
            scaled[k * 128 : (k + 1) * 128, lane : lane + 128] = (own * fac).astype(BF16)

    def base(x_of, z_of):
        return (x_of * NZ + z_of) * BLOCK

    def multiply(p):
        def one(i, _):
            row = pl.multiple_of(base(i, zeta(z, p)), 32)
            part[pl.ds(row, BLOCK), :] = jnp.dot(at[pl.ds(row, BLOCK), :], scaled[...], preferred_element_type=F32)
            return 0

        lax.fori_loop(0, NX, one, 0)

    def at_row(row, r):
        return pl.ds(pl.multiple_of(row + r, 16), 16)

    def pieces(rows):
        return range(0, rows, 16)

    def loop(count, body, carry):
        return body(0, carry) if count == 1 else lax.fori_loop(0, count, body, carry)

    def fold(m, value):
        value = jnp.abs(value)
        for r in range(0, value.shape[0], 8):
            for c in range(0, value.shape[1], 128):
                m = jnp.maximum(m, value[r : r + 8, c : c + 128])
        return m

    def spread(scale):
        return jnp.concatenate([scale] * (KV // 2 // 128), axis=1)

    def encode(row_of, blocks, count, code, scale_ref, add=None):
        def largest(b, m):
            for r in pieces(count):
                value = part[at_row(row_of(b), r), :]
                if add is not None:
                    value = value + add(b, r)
                    part[at_row(row_of(b), r), :] = value
                m = fold(m, value)
            return m

        m = loop(blocks, largest, jnp.zeros((8, 128), F32))
        m = jnp.maximum(jnp.max(m, axis=0, keepdims=True), TINY)
        scale_ref[...] = jnp.broadcast_to(m * (1.0 / TOP), (8, 128))
        inverse = spread(TOP / m)

        def put(b, _):
            for r in pieces(count):
                value = part[at_row(row_of(b), r), :]
                code[at_row(b * count, r), :] = jnp.round(value * inverse).astype(jnp.int32).astype(I16)
            return 0

        loop(blocks, put, 0)

    def adder(count, code, scale_ref):
        scale = spread(scale_ref[0:1, :])
        return lambda b, r: code[at_row(b * count, r), :].astype(jnp.int32).astype(F32) * scale

    def message(bufs, there, here, slot, kind, recv_sem, peer):
        code, got, scale, got_scale = bufs
        one = (slice(0, 1),)
        return [
            pltpu.make_async_remote_copy(
                code.at[here], got.at[there], sent.at[kind, 0], recv_sem.at[slot + (0,)], device_id=peer, device_id_type=MESH
            ),
            pltpu.make_async_remote_copy(
                scale.at[here + one], got_scale.at[there + one], sent.at[kind, 1], recv_sem.at[slot + (1,)],
                device_id=peer, device_id_type=MESH,
            ),
        ]

    def start(copies):
        for copy in copies:
            copy.start()

    def landed(copies):
        for copy in copies:
            copy.wait_recv()

    def drain(bufs, kind):
        everything = (slice(None),) * (len(bufs[2].shape) - 2)
        for i, ref in enumerate((bufs[0], bufs[2].at[everything + (slice(0, 1),)])):
            pltpu.make_async_remote_copy(
                ref, ref, sent.at[kind, i], sent.at[kind, i], device_id=at_x(1), device_id_type=MESH
            ).wait_send()

    class Ring:
        def __init__(self, half, first, bufs, recv_sem, kind):
            self.half, self.first, self.bufs, self.recv_sem, self.kind = half, first, bufs, recv_sem, kind

        def copies(self, p, way, late):
            units = (p, way, pl.ds(2, 1) if late else pl.ds(0, 2))
            return message(self.bufs, units, units, (p, way, late), self.kind, self.recv_sem, at_x(1 + 2 * way))

        def row(self, step, z_of, half):
            return base((x + step) % NX, z_of) + self.first + half * self.half

        def own(self, p, z_of):
            def one(way, _):
                for unit in range(2):
                    row = self.row(1 + 2 * way, z_of, 1 - way) if unit else self.row(2, z_of, way)
                    encode(lambda b: row, 1, self.half, self.bufs[0].at[p, way, unit], self.bufs[2].at[p, way, unit])
                start(self.copies(p, way, 0))
                return 0

            lax.fori_loop(0, 2, one, 0)

        def pass_on(self, p, z_of):
            def one(way, _):
                landed(self.copies(p, way, 0))
                row = self.row(1 + 2 * way, z_of, way)
                encode(
                    lambda b: row, 1, self.half, self.bufs[0].at[p, way, 2], self.bufs[2].at[p, way, 2],
                    adder(self.half, self.bufs[1].at[p, way, 0], self.bufs[3].at[p, way, 0]),
                )
                start(self.copies(p, way, 1))
                return 0

            lax.fori_loop(0, 2, one, 0)

        def finish(self, p, z_of, put):
            for way in range(2):
                landed(self.copies(p, way, 1))

            def one(half, _):
                one = adder(self.half, self.bufs[1].at[p, half, 2], self.bufs[3].at[p, half, 2])
                two = adder(self.half, self.bufs[1].at[p, 1 - half, 1], self.bufs[3].at[p, 1 - half, 1])
                row = self.row(0, z_of, half)
                for r in pieces(self.half):
                    put(row, half, r, part[at_row(row, r), :] + one(0, r) + two(0, r))
                return 0

            lax.fori_loop(0, 2, one, 0)

    class Chain:
        def __init__(self, half, first, x_of, blocks, bufs, recv_sem, kind):
            self.half, self.first, self.x_of, self.blocks = half, first, x_of, blocks
            self.bufs, self.recv_sem, self.kind = bufs, recv_sem, kind

        def copies(self, p, half, slot):
            step = (1 if half == 0 else NZ - 1) if p == 0 else (1 if p % 2 else NZ - 1)
            return message(self.bufs, (slot, half), (p, half), (slot, half), self.kind, self.recv_sem, at_z(step))

        def begin(self):
            for half in range(2):
                self.hop(0, half)

        def hop(self, p, half):
            takes = p >= 3 or (p >= 1 and half == 1 - p % 2)
            if takes:
                landed(self.copies(p, half, p - 1))

            def row_of(b):
                return base(self.x_of(b), zeta(z, p)) + self.first + half * self.half

            encode(
                row_of, self.blocks, self.half, self.bufs[0].at[p, half], self.bufs[2].at[p, half],
                adder(self.half, self.bufs[1].at[p - 1, half], self.bufs[3].at[p - 1, half]) if takes else None,
            )
            start(self.copies(p, half, p + 1 if p else half))

        def finish(self, put):
            for half in range(2):
                for slot in (NZ - 2, NZ - 1):
                    landed(self.copies(0, half, slot))
                one, two = (
                    adder(self.half, self.bufs[1].at[slot, half], self.bufs[3].at[slot, half]) for slot in (NZ - 2, NZ - 1)
                )

                def block(b, _):
                    row = base(self.x_of(b), z) + self.first + half * self.half
                    for r in pieces(self.half):
                        put(row, half, r, part[at_row(row, r), :] + one(b, r) + two(b, r))
                    return 0

                loop(self.blocks, block, 0)

    ring1 = Ring(H1, 0, (xs1, xr1, xss1, xrs1), x1_recv, 0)
    chain1 = Chain(H1, 0, lambda b: x, 1, (zs1, zr1, zss1, zrs1), z1_recv, 1)
    ring2 = Ring(H2, ROWS1, (xs2, xr2, xss2, xrs2), x2_recv, 2)
    chain2 = Chain(H2, ROWS1, lambda b: b, NX, (zs2, zr2, zss2, zrs2), z2_recv, 3)

    def keep(row, half, r, value):
        part[at_row(row, r), :] = value

    def put1(row, half, r, value):
        out_ref[half * H1 + r : half * H1 + r + 16, :] = value

    def put2(row, half, r, value):
        out_ref[at_row(ROWS1 + half * H2, r), :] = value

    for task in ORDER:
        kind, p = task[0], int(task[1:2] or 0)
        if kind == "M":
            multiply(p)
        elif kind == "A":
            ring1.own(p, zeta(z, p))
        elif kind == "B":
            ring1.pass_on(p, zeta(z, p))
        elif kind == "C":
            ring1.finish(p, zeta(z, p), keep)
        elif kind == "Z":
            chain1.hop(p, p % 2)
            chain1.hop(p, 1 - p % 2)
        elif kind == "H" and p == 0:
            chain2.begin()
        elif kind == "H":
            chain2.hop(p, p % 2 if task[2] == "0" else 1 - p % 2)
        elif kind == "E":
            chain2.finish(keep)
        elif kind == "F":
            ring2.own(0, z)
        elif kind == "G":
            ring2.pass_on(0, z)
        elif kind == "I":
            ring2.finish(0, z, put2)
    chain1.finish(put1)

    gp_copy.wait_send()
    pltpu.make_async_remote_copy(
        norms.at[0:7], norms.at[0:7], n_send, n_send, device_id=at_x(1), device_id_type=MESH
    ).wait_send()
    for chain_or_ring in (ring1, chain1, ring2, chain2):
        drain(chain_or_ring.bufs, chain_or_ring.kind)


def per_device(activations, cotangents, doc_ids):
    length, half_kv = activations.shape[1], cotangents.shape[2]
    sections = lax.axis_size("section")
    dma = pltpu.SemaphoreType.DMA
    units1, units2 = (STEPS, 2, 3), (1, 2, 3)
    hops, slots = (STEPS - 1, 2), (STEPS, 2)

    def buffers(ours, theirs, rows):
        return [pltpu.VMEM(s + (rows, half_kv), I16) for s in (ours, theirs)] + [
            pltpu.VMEM(s + (8, 128), F32) for s in (ours, theirs)
        ]

    grad, clip = pl.pallas_call(
        kernel,
        out_shape=(
            jax.ShapeDtypeStruct((BLOCK, half_kv), F32),
            jax.ShapeDtypeStruct((1, DOCS), F32),
        ),
        in_specs=[
            pl.BlockSpec(memory_space=pl.ANY),
            pl.BlockSpec(memory_space=pl.ANY),
            pl.BlockSpec(memory_space=pltpu.VMEM),
        ],
        out_specs=[pl.BlockSpec(memory_space=pltpu.VMEM)] * 2,
        scratch_shapes=[
            pltpu.VMEM((length, D), BF16),
            pltpu.VMEM((D, length), BF16),
            pltpu.VMEM((length, half_kv), BF16),
            pltpu.VMEM((length, half_kv), BF16),
            pltpu.VMEM((D, half_kv), F32),
            pltpu.VMEM((length, half_kv), BF16),
            pltpu.VMEM((2 * sections + length // 128, DOCS, 128), F32),
            pltpu.VMEM((2, 384, 256), F32),
            pltpu.VMEM((2, 384, 256), F32),
            *buffers(units1, units1, H1),
            *buffers(hops, slots, H1),
            *buffers(units2, units2, H2),
            *buffers(hops, slots, NX * H2),
            dma((D // K_CHUNK + 3,)),
            dma(()),
            dma((2,)),
            dma(()),
            dma((7,)),
            dma((4, 2)),
            dma((STEPS, 2, 2, 2)),
            dma(slots + (2,)),
            dma((1, 2, 2, 2)),
            dma(slots + (2,)),
        ],
        compiler_params=pltpu.CompilerParams(
            collective_id=0, has_side_effects=True, vmem_limit_bytes=63 << 20
        ),
        name="clip_and_reduce",
    )(activations[0], cotangents[0], doc_ids)
    return grad[None], clip


def solution(mesh):
    return jax.shard_map(
        per_device,
        mesh=mesh,
        in_specs=(P("section", "dp", None), P("section", "dp", "tensor"), P("dp", None)),
        out_specs=(P("section", "dp", "tensor"), P("dp", None)),
        check_vma=False,
    )
```

time: 69.9 us -> 60.1 us (0.86)
  Pallas kernels: 66.3 us -> 56.5 us
    pallas_call x1, Pallas kernels: 66.3 us -> 56.5 us  [per_device(): pl.pallas_call(kernel, out_shape=(jax.ShapeDtypeStruct((BLOCK, half_kv),...]
where the time goes in v2:
time: 60.1 us; the launch traced here: 59.9 us
  Pallas kernels  56.5 us (94%)
  local copies, waits for them, and re-layouts  2.83 us (5%)
  between operations  0.64 us (1%)
    pallas_call x1, Pallas kernels, per_device(): pl.pallas_call(kernel, out_shape=(jax.ShapeDtypeStruct((BLOCK, half_kv),...  56.5 us
    unnamed x2, local copies, waits for them, and re-layouts  2.83 us

profile of v2, /device:TPU:2, one launch (start us, length us, event | category | flops | bytes accessed | tf_op | source)
XLA Modules:
  0.0 59.9 jit_solution(13330565321135573827)
XLA Ops:
  0.6 56.5 %clip_and_reduce.1 = (f32[160,512]{1,0:T(8,128)}, f32[1,16]{1,0:T(1,128)}) custom-call(bf16[1024,5120]{1,0:T(8,128)(2,1)} %bitcast.3, bf16[1024,512]{1,0:T(8,128)(2,1)} %bitcast.4, s32[1,1024]{1,0:T(1,128)} %ids_ref.1), custom_call_target="tpu_custom_call" | custom-call | tf_op jit(solution)/shard_map/clip_and_reduce/pallas_call | solution.py:415
  57.1 1.7 %copy.7 = f32[1,160,512]{2,1,0:T(8,128)} copy(f32[1,160,512]{2,1,0:T(8,128)} %bitcast.5) | data formatting | bytes 655360
  58.8 1.1 %copy.8 = f32[1,16]{1,0:T(1,128)} copy(f32[1,16]{1,0:T(1,128)} %get-tuple-element.9) | data formatting | bytes 128

commit v3 on v2

--- a/solution.py
+++ b/solution.py
@@ -26,6 +26,7 @@
 H1, H2 = ROWS1 // 2, ROWS2 // 2
 STEPS = NZ
 K_CHUNK = 1280
+UNROLL = 4
 TRANSPOSE_EARLY = True
 ORDER = (
     "M0", "A0", "H00", "M1", "H10", "A1", "M2", "H20", "A2", "M3", "B0", "A3", "M4", "H11", "H21", "A4", "M5", "B1", "M6",
@@ -48,8 +49,8 @@
 
 
 def kernel(
-    a_hbm, g_hbm, ids_ref, out_ref, clip_ref,
-    a, at, g, gp, part, scaled, norms, acts, cots,
+    a_hbm, g_hbm, ids_ref, out_ref,
+    a, at, g, gp, part, scaled, norms, acts, cots, ruler,
     xs1, xr1, xss1, xrs1, zs1, zr1, zss1, zrs1,
     xs2, xr2, xss2, xrs2, zs2, zr2, zss2, zrs2,
     a_sem, g_sem, gp_sem, n_send, n_recv, sent, x1_recv, z1_recv, x2_recv, z2_recv,
@@ -66,10 +67,6 @@
         return (y, x * NZ + (z + step) % NZ, core)
 
     group = [((y + i) % sections, dp, (core + j) % 2) for i in range(4) for j in range(2) if i or j]
-    barrier = pltpu.get_barrier_semaphore()
-    for peer in group + [at_x(1), at_x(NX - 1), at_z(1), at_z(NZ - 1)]:
-        pl.semaphore_signal(barrier, inc=1, device_id=peer, device_id_type=MESH)
-
     chunks = D // K_CHUNK
     first = pl.multiple_of(384 * core, 128)
     rest = pl.multiple_of(640 * (1 - core), 128)
@@ -85,25 +82,27 @@
     g_copy.start()
     for k in range(2):
         a_copy(k).start()
-    pl.semaphore_wait(barrier, len(group) + 4)
+
+    barrier = pltpu.get_barrier_semaphore()
+    for peer in group + [at_x(1), at_x(NX - 1), at_z(1), at_z(NZ - 1)]:
+        pl.semaphore_signal(barrier, inc=1, device_id=peer, device_id_type=MESH)
+
+    one_hot = (lax.broadcasted_iota(jnp.int32, (DOCS, length), 0) == ids_ref[...]).astype(F32)
+    for k in range(length // 128):
+        norms[2 * sections + k] = one_hot[:, k * 128 : (k + 1) * 128]
+
+    def hot(start, count):
+        return jnp.concatenate([norms[2 * sections + start + k] for k in range(count)], axis=1)
+
+    def tokens(j):
+        u0 = pl.multiple_of(512 * core + 256 * j, 128)
+        return pl.multiple_of(jnp.maximum(u0 - 128, 0), 128), u0
 
     other_row = pl.multiple_of(384 * (1 - core), 128)
     gp_copy = pltpu.make_async_remote_copy(
         g_hbm.at[pl.ds(other_row, 640)], gp.at[pl.ds(other_row, 640)], gp_sem.at[0], gp_sem.at[1],
         device_id=(y, dp, 1 - core), device_id_type=MESH,
     )
-    gp_copy.start()
-
-    one_hot = (lax.broadcasted_iota(jnp.int32, (DOCS, length), 0) == ids_ref[...]).astype(F32)
-    for k in range(length // 128):
-        norms[2 * sections + k] = one_hot[:, k * 128 : (k + 1) * 128]
-
-    def hot(start, count):
-        return jnp.concatenate([norms[2 * sections + start + k] for k in range(count)], axis=1)
-
-    def tokens(j):
-        u0 = pl.multiple_of(512 * core + 256 * j, 128)
-        return pl.multiple_of(jnp.maximum(u0 - 128, 0), 128), u0
 
     g_copy.wait()
     for j in range(2):
@@ -117,6 +116,9 @@
         elif k + 2 == chunks:
             for i in range(3):
                 a_copy(chunks + i).start()
+        if k == 1:
+            pl.semaphore_wait(barrier, len(group) + 4)
+            gp_copy.start()
         column = k * K_CHUNK
         for j in range(2):
             t0, u0 = tokens(j)
@@ -167,7 +169,7 @@
     norm_sq = jnp.broadcast_to(jnp.sum(norm_sq, axis=1, keepdims=True), (DOCS, 128))
     bound = math.sqrt(4.0 * CLIP_TOK * sections * D * KV)
     clip = jnp.minimum(1.0, bound * lax.rsqrt(norm_sq + 1e-06))
-    clip_ref[...] = clip.T[:1, :]
+    out_ref[BLOCK : BLOCK + DOCS, :128] = clip
     factor = clip * (1.0 / math.sqrt(NX * NZ * length))
     for k in range(length // 128):
         fac = tn(norms[2 * sections + k], factor, lax.Precision.HIGHEST)
@@ -184,7 +186,7 @@
             part[pl.ds(row, BLOCK), :] = jnp.dot(at[pl.ds(row, BLOCK), :], scaled[...], preferred_element_type=F32)
             return 0
 
-        lax.fori_loop(0, NX, one, 0)
+        lax.fori_loop(0, NX, one, 0, unroll=UNROLL)
 
     def at_row(row, r):
         return pl.ds(pl.multiple_of(row + r, 16), 16)
@@ -237,10 +239,10 @@
         one = (slice(0, 1),)
         return [
             pltpu.make_async_remote_copy(
-                code.at[here], got.at[there], sent.at[kind, 0], recv_sem.at[slot + (0,)], device_id=peer, device_id_type=MESH
+                code.at[here], got.at[there], sent.at[kind, 0], recv_sem.at[slot], device_id=peer, device_id_type=MESH
             ),
             pltpu.make_async_remote_copy(
-                scale.at[here + one], got_scale.at[there + one], sent.at[kind, 1], recv_sem.at[slot + (1,)],
+                scale.at[here + one], got_scale.at[there + one], sent.at[kind, 1], recv_sem.at[slot],
                 device_id=peer, device_id_type=MESH,
             ),
         ]
@@ -249,9 +251,11 @@
         for copy in copies:
             copy.start()
 
-    def landed(copies):
-        for copy in copies:
-            copy.wait_recv()
+    def landed(rows, recv_sem):
+        here = ruler.at[pl.ds(0, rows)]
+        pltpu.make_async_remote_copy(
+            here, here, recv_sem, recv_sem, device_id=at_x(1), device_id_type=MESH
+        ).wait_recv()
 
     def drain(bufs, kind):
         everything = (slice(None),) * (len(bufs[2].shape) - 2)
@@ -267,6 +271,9 @@
         def copies(self, p, way, late):
             units = (p, way, pl.ds(2, 1) if late else pl.ds(0, 2))
             return message(self.bufs, units, units, (p, way, late), self.kind, self.recv_sem, at_x(1 + 2 * way))
+
+        def landed(self, p, way, late):
+            landed((2 - late) * (2 * self.half + 1), self.recv_sem.at[p, way, late])
 
         def row(self, step, z_of, half):
             return base((x + step) % NX, z_of) + self.first + half * self.half
@@ -283,7 +290,7 @@
 
         def pass_on(self, p, z_of):
             def one(way, _):
-                landed(self.copies(p, way, 0))
+                self.landed(p, way, 0)
                 row = self.row(1 + 2 * way, z_of, way)
                 encode(
                     lambda b: row, 1, self.half, self.bufs[0].at[p, way, 2], self.bufs[2].at[p, way, 2],
@@ -296,7 +303,7 @@
 
         def finish(self, p, z_of, put):
             for way in range(2):
-                landed(self.copies(p, way, 1))
+                self.landed(p, way, 1)
 
             def one(half, _):
                 one = adder(self.half, self.bufs[1].at[p, half, 2], self.bufs[3].at[p, half, 2])
@@ -317,6 +324,9 @@
             step = (1 if half == 0 else NZ - 1) if p == 0 else (1 if p % 2 else NZ - 1)
             return message(self.bufs, (slot, half), (p, half), (slot, half), self.kind, self.recv_sem, at_z(step))
 
+        def landed(self, slot, half):
+            landed(2 * self.blocks * self.half + 1, self.recv_sem.at[slot, half])
+
         def begin(self):
             for half in range(2):
                 self.hop(0, half)
@@ -324,7 +334,7 @@
         def hop(self, p, half):
             takes = p >= 3 or (p >= 1 and half == 1 - p % 2)
             if takes:
-                landed(self.copies(p, half, p - 1))
+                self.landed(p - 1, half)
 
             def row_of(b):
                 return base(self.x_of(b), zeta(z, p)) + self.first + half * self.half
@@ -338,7 +348,7 @@
         def finish(self, put):
             for half in range(2):
                 for slot in (NZ - 2, NZ - 1):
-                    landed(self.copies(0, half, slot))
+                    self.landed(slot, half)
                 one, two = (
                     adder(self.half, self.bufs[1].at[slot, half], self.bufs[3].at[slot, half]) for slot in (NZ - 2, NZ - 1)
                 )
@@ -400,6 +410,11 @@
         drain(chain_or_ring.bufs, chain_or_ring.kind)
 
 
+def take_apart(result_ref, grad_ref, clip_ref):
+    grad_ref[0] = result_ref[:BLOCK, :]
+    clip_ref[...] = result_ref[BLOCK:, :128].T[:1, :]
+
+
 def per_device(activations, cotangents, doc_ids):
     length, half_kv = activations.shape[1], cotangents.shape[2]
     sections = lax.axis_size("section")
@@ -412,18 +427,15 @@
             pltpu.VMEM(s + (8, 128), F32) for s in (ours, theirs)
         ]
 
-    grad, clip = pl.pallas_call(
+    result = pl.pallas_call(
         kernel,
-        out_shape=(
-            jax.ShapeDtypeStruct((BLOCK, half_kv), F32),
-            jax.ShapeDtypeStruct((1, DOCS), F32),
-        ),
+        out_shape=jax.ShapeDtypeStruct((BLOCK + DOCS, half_kv), F32),
         in_specs=[
             pl.BlockSpec(memory_space=pl.ANY),
             pl.BlockSpec(memory_space=pl.ANY),
             pl.BlockSpec(memory_space=pltpu.VMEM),
         ],
-        out_specs=[pl.BlockSpec(memory_space=pltpu.VMEM)] * 2,
+        out_specs=pl.BlockSpec(memory_space=pltpu.VMEM),
         scratch_shapes=[
             pltpu.VMEM((length, D), BF16),
             pltpu.VMEM((D, length), BF16),
@@ -434,6 +446,7 @@
             pltpu.VMEM((2 * sections + length // 128, DOCS, 128), F32),
             pltpu.VMEM((2, 384, 256), F32),
             pltpu.VMEM((2, 384, 256), F32),
+            pltpu.VMEM((2 * NX * H2 + 8, 128), F32),
             *buffers(units1, units1, H1),
             *buffers(hops, slots, H1),
             *buffers(units2, units2, H2),
@@ -444,17 +457,26 @@
             dma(()),
             dma((7,)),
             dma((4, 2)),
-            dma((STEPS, 2, 2, 2)),
-            dma(slots + (2,)),
-            dma((1, 2, 2, 2)),
-            dma(slots + (2,)),
+            dma((STEPS, 2, 2)),
+            dma(slots),
+            dma((1, 2, 2)),
+            dma(slots),
         ],
         compiler_params=pltpu.CompilerParams(
             collective_id=0, has_side_effects=True, vmem_limit_bytes=63 << 20
         ),
         name="clip_and_reduce",
     )(activations[0], cotangents[0], doc_ids)
-    return grad[None], clip
+    return pl.pallas_call(
+        take_apart,
+        out_shape=(
+            jax.ShapeDtypeStruct((1, BLOCK, half_kv), F32),
+            jax.ShapeDtypeStruct((1, DOCS), F32),
+        ),
+        in_specs=[pl.BlockSpec(memory_space=pltpu.VMEM)],
+        out_specs=[pl.BlockSpec(memory_space=pltpu.VMEM)] * 2,
+        name="take_apart",
+    )(result)
 
 
 def solution(mesh):

time: 60.1 us -> 55.6 us (0.925)
  local copies, waits for them, and re-layouts: 2.83 us -> 0 us
  Pallas kernels: 56.5 us -> 54.8 us
    unnamed x2 -> x0, local copies, waits for them, and re-layouts: 2.83 us -> none
    pallas_call x1 -> x2, Pallas kernels: 56.5 us -> 54.8 us  [the longest x1 53 us: per_device(): pl.pallas_call(kernel, out_shape=jax.ShapeDtypeStruct((BLOCK + DOCS, half...]
where the time goes in v3:
time: 55.6 us; the launch traced here: 55.4 us
  Pallas kernels  54.8 us (99%)
  between operations  0.64 us (1%)
    pallas_call x1, Pallas kernels, per_device(): pl.pallas_call(kernel, out_shape=jax.ShapeDtypeStruct((BLOCK + DOCS, half...  53 us
    pallas_call x1, Pallas kernels, per_device(): pl.pallas_call(take_apart, out_shape=(jax.ShapeDtypeStruct((1, BLOCK, hal...  1.73 us

profile of v3, /device:TPU:2, one launch (start us, length us, event | category | flops | bytes accessed | tf_op | source)
XLA Modules:
  0.0 55.4 jit_solution(1505412491282924287)
XLA Ops:
  0.6 53.0 %clip_and_reduce.1.result_ref = f32[176,512]{1,0:T(8,128)} custom-call(bf16[1024,5120]{1,0:T(8,128)(2,1)} %bitcast.2, bf16[1024,512]{1,0:T(8,128)(2,1)} %bitcast.3, s32[1,1024]{1,0:T(1,128)} %ids_ref.1), custom_call_target="tpu_custom_call" | custom-call | tf_op jit(solution)/shard_map/clip_and_reduce/pallas_call | solution.py:430
  53.7 1.7 %take_apart.1 = (f32[1,160,512]{2,1,0:T(8,128)}, f32[1,16]{1,0:T(1,128)}) custom-call(f32[176,512]{1,0:T(8,128)} %clip_and_reduce.1.result_ref), custom_call_target="tpu_custom_call" | custom-call | tf_op jit(solution)/shard_map/take_apart/pallas_call | solution.py:470

commit v4 on v3

--- a/solution.py
+++ b/solution.py
@@ -26,12 +26,12 @@
 H1, H2 = ROWS1 // 2, ROWS2 // 2
 STEPS = NZ
 K_CHUNK = 1280
-UNROLL = 4
+AHEAD = 3
 TRANSPOSE_EARLY = True
 ORDER = (
-    "M0", "A0", "H00", "M1", "H10", "A1", "M2", "H20", "A2", "M3", "B0", "A3", "M4", "H11", "H21", "A4", "M5", "B1", "M6",
-    "H30", "B2", "A5", "H40", "M7", "C0", "Z0", "A7", "A6", "H31", "H41", "B3", "H50", "H60", "B4", "C1", "Z1", "C2", "Z2",
-    "H51", "H61", "B5", "B7", "B6", "C3", "Z3", "C4", "Z4", "E", "F", "C5", "C7", "Z5", "C6", "Z6", "G", "I",
+    "P", "H00", "M1", "A1", "H10", "M2", "H20", "A2", "M3", "M4", "B0", "A4", "A3", "M5", "H21", "H11", "M6", "M7", "H30",
+    "H40", "B1", "B2", "A6", "A5", "A7", "C0", "Z0", "H41", "H31", "B4", "B3", "H60", "H50", "C1", "Z1", "C2", "Z2", "H61",
+    "H51", "B6", "B5", "B7", "C4", "Z4", "C3", "Z3", "C6", "E", "F", "C5", "C7", "Z6", "Z5", "G", "I",
 )
 
 
@@ -80,7 +80,7 @@
 
     g_copy = pltpu.make_async_copy(g_hbm, g, g_sem)
     g_copy.start()
-    for k in range(2):
+    for k in range(AHEAD):
         a_copy(k).start()
 
     barrier = pltpu.get_barrier_semaphore()
@@ -111,9 +111,9 @@
 
     for k in range(chunks):
         a_copy(k).wait()
-        if k + 2 < chunks:
-            a_copy(k + 2).start()
-        elif k + 2 == chunks:
+        if k + AHEAD < chunks:
+            a_copy(k + AHEAD).start()
+        elif k + AHEAD == chunks:
             for i in range(3):
                 a_copy(chunks + i).start()
         if k == 1:
@@ -159,7 +159,7 @@
         at[pl.ds(lane, 128), pl.ds(rest, 384)] = a[pl.ds(rest, 384), pl.ds(lane, 128)].T
         return 0
 
-    lax.fori_loop(0, D // 128, transpose, 0)
+    lax.fori_loop(0, D // 128, transpose, 0, unroll=4)
 
     for copy in n_copies:
         copy.wait_recv()
@@ -180,13 +180,10 @@
     def base(x_of, z_of):
         return (x_of * NZ + z_of) * BLOCK
 
-    def multiply(p):
-        def one(i, _):
-            row = pl.multiple_of(base(i, zeta(z, p)), 32)
+    def multiply(p, steps=(0, 1, 2, 3)):
+        for step in steps:
+            row = pl.multiple_of(base((x + step) % NX, zeta(z, p)), 32)
             part[pl.ds(row, BLOCK), :] = jnp.dot(at[pl.ds(row, BLOCK), :], scaled[...], preferred_element_type=F32)
-            return 0
-
-        lax.fori_loop(0, NX, one, 0, unroll=UNROLL)
 
     def at_row(row, r):
         return pl.ds(pl.multiple_of(row + r, 16), 16)
@@ -279,14 +276,14 @@
             return base((x + step) % NX, z_of) + self.first + half * self.half
 
         def own(self, p, z_of):
-            def one(way, _):
-                for unit in range(2):
-                    row = self.row(1 + 2 * way, z_of, 1 - way) if unit else self.row(2, z_of, way)
-                    encode(lambda b: row, 1, self.half, self.bufs[0].at[p, way, unit], self.bufs[2].at[p, way, unit])
-                start(self.copies(p, way, 0))
-                return 0
-
-            lax.fori_loop(0, 2, one, 0)
+            lax.fori_loop(0, 2, lambda way, _: self.own_way(p, z_of, way), 0)
+
+        def own_way(self, p, z_of, way):
+            for unit in range(2):
+                row = self.row(1 + 2 * way, z_of, 1 - way) if unit else self.row(2, z_of, way)
+                encode(lambda b: row, 1, self.half, self.bufs[0].at[p, way, unit], self.bufs[2].at[p, way, unit])
+            start(self.copies(p, way, 0))
+            return 0
 
         def pass_on(self, p, z_of):
             def one(way, _):
@@ -377,7 +374,13 @@
 
     for task in ORDER:
         kind, p = task[0], int(task[1:2] or 0)
-        if kind == "M":
+        if kind == "P":
+            multiply(0, (2, 1))
+            ring1.own_way(0, zeta(z, 0), 0)
+            multiply(0, (3,))
+            ring1.own_way(0, zeta(z, 0), 1)
+            multiply(0, (0,))
+        elif kind == "M":
             multiply(p)
         elif kind == "A":
             ring1.own(p, zeta(z, p))
@@ -410,9 +413,14 @@
         drain(chain_or_ring.bufs, chain_or_ring.kind)
 
 
-def take_apart(result_ref, grad_ref, clip_ref):
-    grad_ref[0] = result_ref[:BLOCK, :]
-    clip_ref[...] = result_ref[BLOCK:, :128].T[:1, :]
+def take_apart(result_ref, grad_ref, clip_ref, clip, grad_sem, clip_sem):
+    grad_copy = pltpu.make_async_copy(result_ref.at[pl.ds(0, BLOCK)], grad_ref.at[0], grad_sem)
+    grad_copy.start()
+    clip_copy = pltpu.make_async_copy(result_ref.at[pl.ds(BLOCK, DOCS), pl.ds(0, 128)], clip, clip_sem)
+    clip_copy.start()
+    clip_copy.wait()
+    clip_ref[...] = clip[...].T[:1, :]
+    grad_copy.wait()
 
 
 def per_device(activations, cotangents, doc_ids):
@@ -429,7 +437,7 @@
 
     result = pl.pallas_call(
         kernel,
-        out_shape=jax.ShapeDtypeStruct((BLOCK + DOCS, half_kv), F32),
+        out_shape=pltpu.VMEM((BLOCK + DOCS, half_kv), F32),
         in_specs=[
             pl.BlockSpec(memory_space=pl.ANY),
             pl.BlockSpec(memory_space=pl.ANY),
@@ -473,8 +481,14 @@
             jax.ShapeDtypeStruct((1, BLOCK, half_kv), F32),
             jax.ShapeDtypeStruct((1, DOCS), F32),
         ),
-        in_specs=[pl.BlockSpec(memory_space=pltpu.VMEM)],
-        out_specs=[pl.BlockSpec(memory_space=pltpu.VMEM)] * 2,
+        in_specs=[pl.BlockSpec(memory_space=pl.ANY)],
+        out_specs=[pl.BlockSpec(memory_space=pl.ANY), pl.BlockSpec(memory_space=pltpu.VMEM)],
+        scratch_shapes=[
+            pltpu.VMEM((DOCS, 128), F32),
+            pltpu.SemaphoreType.DMA(()),
+            pltpu.SemaphoreType.DMA(()),
+        ],
+        compiler_params=pltpu.CompilerParams(vmem_limit_bytes=1 << 20),
         name="take_apart",
     )(result)
 

time: 55.6 us -> 53.8 us (0.968)
  Pallas kernels: 54.8 us -> 52.9 us
    pallas_call x1, Pallas kernels: 53 us -> 51.6 us  [per_device(): pl.pallas_call(kernel, out_shape=pltpu.VMEM((BLOCK + DOCS, half_kv), F32)...]
where the time goes in v4:
time: 53.8 us; the launch traced here: 53.7 us
  Pallas kernels  52.9 us (98%)
  between operations  0.8 us (1%)
    pallas_call x1, Pallas kernels, per_device(): pl.pallas_call(kernel, out_shape=pltpu.VMEM((BLOCK + DOCS, half_kv), F32)...  51.6 us
    pallas_call x1, Pallas kernels, per_device(): pl.pallas_call(take_apart, out_shape=(jax.ShapeDtypeStruct((1, BLOCK, hal...  1.25 us

profile of v4, /device:TPU:2, one launch (start us, length us, event | category | flops | bytes accessed | tf_op | source)
XLA Modules:
  0.0 53.7 jit_solution(8566566342408240995)
XLA Ops:
  0.6 51.6 %clip_and_reduce.1.result_ref = f32[176,512]{1,0:T(8,128)S(1)} custom-call(bf16[1024,5120]{1,0:T(8,128)(2,1)} %bitcast.2, bf16[1024,512]{1,0:T(8,128)(2,1)} %bitcast.3, s32[1,1024]{1,0:T(1,128)} %ids_ref.1), custom_call_target="tpu_custom_call" | custom-call | tf_op jit(solution)/shard_map/clip_and_reduce/pallas_call | solution.py:438
  52.3 1.3 %take_apart.1 = (f32[1,160,512]{2,1,0:T(8,128)}, f32[1,16]{1,0:T(1,128)}) custom-call(f32[176,512]{1,0:T(8,128)S(1)} %clip_and_reduce.1.result_ref), custom_call_target="tpu_custom_call" | custom-call | tf_op jit(solution)/shard_map/take_apart/pallas_call | solution.py:478
